TPU v7x, 32 devices: a whole 2x2x4 slice. The times are simulated.
32 devices in a mesh: dp: 8 (over z, y), tensor: 4 (over x, core).
Axes of the slice: x: 2, y: 2, z: 4, core: 2. Of those that a mesh axis runs over, the one named last changes fastest.
Arguments:
- layer_input: bfloat16 [196, 64, 768], P('tensor', 'dp'), may hold values from -6 to 6
- image_counts: int32 [8], P('dp'), may hold values from 4 to 8
- expand: bfloat16 [196, 384], P(None, 'tensor'), may hold values from -0.4375 to 0.4375
- uplift: bfloat16 [384], P('tensor'), may hold values from -3 to 3
- contract: bfloat16 [384, 196], P('tensor'), may hold values from -0.3125 to 0.3125
- offset: bfloat16 [196], P('tensor'), may hold values from -3 to 3
- scaling: bfloat16 [768], replicated, may hold values from 0.099609375 to 1.8984375
- centering: bfloat16 [768], replicated, may hold values from -3 to 3
- rescaling: bfloat16 [768], replicated, may hold values from 0.099609375 to 1.8984375
- recentering: bfloat16 [768], replicated, may hold values from -3 to 3
- broaden: bfloat16 [768, 3072], replicated, may hold values from -0.21875 to 0.21875
- raising: bfloat16 [3072], replicated, may hold values from -3 to 3
- narrow: bfloat16 [3072, 768], replicated, may hold values from -0.109375 to 0.109375
- lowering: bfloat16 [768], replicated, may hold values from -3 to 3
- cotangent: bfloat16 [196, 64, 768], P('tensor', 'dp'), may hold values from -6 to 6
Outputs:
- layer_output: bfloat16 [196, 64, 768], P('tensor', 'dp')
- input_grad: bfloat16 [196, 64, 768], P('tensor', 'dp')
- expand_grad: float32 [196, 384], P(None, 'tensor')
- uplift_grad: float32 [384], P('tensor')
- contract_grad: float32 [384, 196], P('tensor')
- offset_grad: float32 [196], P('tensor')
- scaling_grad: float32 [768], replicated
- centering_grad: float32 [768], replicated
- rescaling_grad: float32 [768], replicated
- recentering_grad: float32 [768], replicated
- broaden_grad: float32 [768, 3072], P(None, ('dp', 'tensor'))
- raising_grad: float32 [3072], P(('dp', 'tensor'))
- narrow_grad: float32 [3072, 768], P(('dp', 'tensor'))
- lowering_grad: float32 [768], replicated
Inputs may be any that keep to these rules, and one draw needn't show every extreme that they name: `image_counts`: slots of a dp index at or above its count hold padding images.
All inputs are finite; a program needn't handle non-finite values.
Results may differ from a plain program's by a relative error of at most 0.007.
Values may be sent and summed in bfloat16 or wider, within the bound.
A program may use at most 128 MiB of HBM per device.

v0:
```python
import jax
import jax.numpy as jnp
from jax import lax
from jax.sharding import PartitionSpec as P


def layer_norm(values, scale_vec, shift_vec):
    centre = values - jnp.mean(values, axis=-1, keepdims=True)
    spread = jnp.mean(centre * centre, axis=-1, keepdims=True)
    return centre * lax.rsqrt(spread + 1e-06) * scale_vec + shift_vec


def local(
    layer_input,
    image_counts,
    expand,
    uplift,
    contract,
    offset,
    scaling,
    centering,
    rescaling,
    recentering,
    broaden,
    raising,
    narrow,
    lowering,
    cotangent,
):
    part_rows, images, model_width = layer_input.shape
    columns = images * model_width
    image_mask = (jnp.arange(images, dtype=jnp.int32) < image_counts[0]).astype(jnp.float32)
    row_mask = jnp.tile(image_mask, part_rows)[:, None]
    input_float = layer_input.astype(jnp.float32)
    normed_first, first_back = jax.vjp(
        layer_norm, input_float, scaling.astype(jnp.float32), centering.astype(jnp.float32)
    )
    normed_local = normed_first.astype(jnp.bfloat16).reshape(part_rows, columns)
    normed_all = lax.all_gather(normed_local, "tensor", axis=0, tiled=True)
    token_pre = (
        jnp.einsum("sj,sn->jn", expand, normed_all, preferred_element_type=jnp.float32)
        + uplift.astype(jnp.float32)[:, None]
    )
    token_act, gelu_token = jax.vjp(jax.nn.gelu, token_pre)
    token_low = token_act.astype(jnp.bfloat16)
    weight_block = contract
    token_out = lax.psum_scatter(
        jnp.einsum("js,jn->sn", weight_block, token_low, preferred_element_type=jnp.float32),
        "tensor",
        scatter_dimension=0,
        tiled=True,
    )
    token_out = token_out + offset.astype(jnp.float32)[:, None]
    mixed_rows = input_float.reshape(part_rows * images, model_width) + token_out.reshape(
        part_rows * images, model_width
    )
    normed_second, second_back = jax.vjp(
        layer_norm, mixed_rows, rescaling.astype(jnp.float32), recentering.astype(jnp.float32)
    )
    normed_low = normed_second.astype(jnp.bfloat16)
    channel_pre = jnp.dot(normed_low, broaden, preferred_element_type=jnp.float32) + raising.astype(
        jnp.float32
    )
    channel_act, gelu_channel = jax.vjp(jax.nn.gelu, channel_pre)
    channel_low = channel_act.astype(jnp.bfloat16)
    channel_out = jnp.dot(
        channel_low, narrow, preferred_element_type=jnp.float32
    ) + lowering.astype(jnp.float32)
    layer_output = (
        ((mixed_rows + channel_out) * row_mask)
        .astype(jnp.bfloat16)
        .reshape(part_rows, images, model_width)
    )
    out_grad = cotangent.astype(jnp.float32).reshape(part_rows * images, model_width) * row_mask
    out_low = out_grad.astype(jnp.bfloat16)
    narrow_grad = jnp.einsum("rk,rd->kd", channel_low, out_low, preferred_element_type=jnp.float32)
    lowering_grad = jnp.sum(out_low.astype(jnp.float32), axis=0)
    act_grad = jnp.einsum("rd,kd->rk", out_low, narrow, preferred_element_type=jnp.float32)
    (pre_grad,) = gelu_channel(act_grad)
    pre_low = pre_grad.astype(jnp.bfloat16)
    broaden_grad = jnp.einsum("rd,rk->dk", normed_low, pre_low, preferred_element_type=jnp.float32)
    raising_grad = jnp.sum(pre_low.astype(jnp.float32), axis=0)
    normed_grad = jnp.einsum("rk,dk->rd", pre_low, broaden, preferred_element_type=jnp.float32)
    rows_grad, rescaling_grad, recentering_grad = second_back(normed_grad)
    mixed_grad = out_grad + rows_grad
    mixed_low = mixed_grad.astype(jnp.bfloat16).reshape(part_rows, columns)
    offset_grad = jnp.sum(mixed_low.astype(jnp.float32), axis=1)
    mixed_all = lax.all_gather(mixed_low, "tensor", axis=0, tiled=True)
    act_token_grad = jnp.einsum(
        "js,sn->jn", contract, mixed_all, preferred_element_type=jnp.float32
    )
    (token_grad,) = gelu_token(act_token_grad)
    token_grad_low = token_grad.astype(jnp.bfloat16)
    expand_grad = jnp.einsum(
        "sn,jn->sj", normed_all, token_grad_low, preferred_element_type=jnp.float32
    )
    contract_grad = jnp.einsum(
        "jn,sn->js", token_low, mixed_all, preferred_element_type=jnp.float32
    )
    uplift_grad = jnp.sum(token_grad_low.astype(jnp.float32), axis=1)
    weight_block = expand
    normed_back = lax.psum_scatter(
        jnp.einsum("sj,jn->sn", weight_block, token_grad_low, preferred_element_type=jnp.float32),
        "tensor",
        scatter_dimension=0,
        tiled=True,
    )
    input_back, scaling_grad, centering_grad = first_back(
        normed_back.reshape(part_rows, images, model_width)
    )
    input_grad = (mixed_grad.reshape(part_rows, images, model_width) + input_back).astype(
        jnp.bfloat16
    )
    expand_grad, uplift_grad, contract_grad, offset_grad = lax.psum(
        (expand_grad, uplift_grad, contract_grad, offset_grad), "dp"
    )
    lowering_grad, scaling_grad, centering_grad, rescaling_grad, recentering_grad = lax.psum(
        (lowering_grad, scaling_grad, centering_grad, rescaling_grad, recentering_grad),
        ("dp", "tensor"),
    )
    broaden_grad, narrow_grad, raising_grad = (
        lax.psum_scatter(broaden_grad, ("dp", "tensor"), scatter_dimension=1, tiled=True),
        lax.psum_scatter(narrow_grad, ("dp", "tensor"), scatter_dimension=0, tiled=True),
        lax.psum_scatter(raising_grad, ("dp", "tensor"), scatter_dimension=0, tiled=True),
    )
    return (
        layer_output,
        input_grad,
        expand_grad,
        uplift_grad,
        contract_grad,
        offset_grad,
        scaling_grad,
        centering_grad,
        rescaling_grad,
        recentering_grad,
        broaden_grad,
        raising_grad,
        narrow_grad,
        lowering_grad,
    )


def solution(mesh):
    in_specs = (
        P("tensor", "dp", None),
        P("dp"),
        P(None, "tensor"),
        P("tensor"),
        P("tensor", None),
        P("tensor"),
        P(),
        P(),
        P(),
        P(),
        P(),
        P(),
        P(),
        P(),
        P("tensor", "dp", None),
    )
    out_specs = (
        P("tensor", "dp", None),
        P("tensor", "dp", None),
        P(None, "tensor"),
        P("tensor"),
        P("tensor", None),
        P("tensor"),
        P(),
        P(),
        P(),
        P(),
        P(None, ("dp", "tensor")),
        P(("dp", "tensor")),
        P(("dp", "tensor"), None),
        P(),
    )
    return jax.shard_map(local, mesh=mesh, in_specs=in_specs, out_specs=out_specs, check_vma=False)
```

profile of v0, /device:TPU:0, one launch (start us, length us, event | category | flops | bytes accessed | tf_op | source)
XLA Modules:
  0.0 556.1 jit_solution(4556848983229731333)
XLA Ops:
  7.3 0.7 convert_element_type.85
  7.9 0.7 convert_element_type.86
  8.6 1.2 convert_reduce_fusion.2
  9.9 1.4 fusion.34
  11.2 1.4 fusion.28
  12.6 1.1 reshape.165
  13.9 29.1 %all-gather.5.cloned.1.call-done = bf16[4,49,6144]{2,1,0:T(8,128)(2,1)} async-done(((bf16[1,49,6144]{2,1,0:T(8,128)(2,1)}), bf16[4,49,6144]{2,1,0:T(8,128)(2,1)}) %all-gather.5.cloned.1.call-update) | async-done | bytes 2408464 | tf_op jit(solution)/shard_map/all_gather | solution.py:39
  42.9 2.5 reshape.166
  46.0 1.4 copy-done.3
  47.4 3.1 convolution_bitcast_fusion.1
  50.6 51.8 %fusion = f32[56,6144]{1,0:T(8,128)} fusion(f32[196,6144]{1,0:T(8,128)} %convolution_bitcast_fusion.1), kind=kCustom, calls=%all-reduce-scatter | all-reduce-scatter fusion | flops 1376257 | bytes 6193664
  102.4 1.1 slice
  103.5 2.1 collective-permute-start
  107.7 8.4 %concatenate = f32[77,6144]{1,0:T(8,128)} concatenate(f32[21,6144]{1,0:T(8,128)} %collective-permute-done, f32[56,6144]{1,0:T(8,128)} %fusion), dimensions={0} | concatenate | bytes 3784704
  116.1 2.7 dynamic-slice_add_fusion
  118.8 2.6 reshape.158
  121.3 1.8 copy.29
  123.9 1.7 add_convert_fusion
  125.6 0.8 copy-done.14
  126.4 4.5 fusion.52
  131.0 5.4 convert_reduce_fusion
  136.5 2.4 multiply_reduce_fusion
  139.6 1.1 copy-done.7
  140.6 1.1 convert_reduce_fusion.4
  141.8 2.2 reshape.167
  144.2 34.2 %all-gather.7.cloned.1.call-done = bf16[4,49,6144]{2,1,0:T(8,128)(2,1)} async-done(((bf16[1,49,6144]{2,1,0:T(8,128)(2,1)}), bf16[4,49,6144]{2,1,0:T(8,128)(2,1)}) %all-gather.7.cloned.1.call-update) | async-done | bytes 2408464 | tf_op jit(solution)/shard_map/all_gather | solution.py:88
  178.4 4.0 reshape.168
  182.4 4.3 fusion.48
  186.7 2.1 convert_reduce_fusion.1
  188.8 1.0 copy-done.9
  189.9 1.7 fusion.53
  191.6 9.4 %fusion.41 = f32[3072,768]{1,0:T(8,128)} fusion(bf16[49,8,768]{2,1,0:T(8,128)(2,1)} %param.29, f32[392]{0:T(512)S(1)} %mul.240, f32[392,3072]{1,0:T(8,128)} %copy-done.25, f32[3072]{0:T(1024)S(1)} %convert_element_type.94), kind=kOutput, calls=%fused_computation.69 | convolution fusion | flops 1862633472 | bytes 14870048 | tf_op jit(solution)/shard_map/rk,rd->kd/dot_general | solution.py:76
  201.1 1.0 copy-done.15
  202.1 8.0 %fusion.54 = f32[768,3072]{0,1:T(8,128)} fusion(bf16[392,768]{1,0:T(8,128)(2,1)S(1)} %copy-done.15, bf16[392,3072]{1,0:T(8,128)(2,1)} %copy-done.24), kind=kOutput, calls=%fused_computation.87 | convolution fusion | flops 1849688064 | bytes 12447744 | tf_op jit(solution)/shard_map/rd,rk->dk/dot_general | solution.py:81
  211.3 3.1 convolution_bitcast_fusion
  214.4 51.0 %fusion.1 = f32[56,6144]{1,0:T(8,128)S(1)} fusion(f32[196,6144]{1,0:T(8,128)} %convolution_bitcast_fusion), kind=kCustom, calls=%all-reduce-scatter.1 | all-reduce-scatter fusion | flops 1376257 | bytes 6193664
  265.4 0.9 slice.1
  266.3 2.4 collective-permute-start.1
  268.6 7.7 %fusion.26 = bf16[49,8,768]{2,1,0:T(8,128)(2,1)} fusion(bf16[3072,768]{1,0:T(8,128)(2,1)} %param.27, f32[392]{0:T(512)S(1)} %mul.240, f32[768]{0:T(1024)S(1)} %convert_element_type.96, f32[392,768]{1,0:T(8,128)S(1)} %copy-done.6, bf16[49,8,768]{2,1,0:T(8,128)(2,1)S(1)} %copy-done.2, f32[392,3072]{1,0:T(8,128)} %copy-done.25, f32[3072]{0:T(1024)S(1)} %convert_element_type.94), kind=kOutput, calls=%fused_computation.46 | convolution fusion | flops 1863536640 | bytes 11960864 | tf_op jit(solution)/shard_map/dot_general | solution.py:66
  276.4 22.0 %all-reduce.6 = (f32[96]{0:T(128)}, f32[49]{0:T(128)}) all-reduce(f32[96]{0:T(128)S(1)} %get-tuple-element.38, f32[49]{0:T(128)S(1)} %reduce_sum.201), channel_id=1, replica_groups=mesh['dp'=8,'tensor'=4] {'dp'}, use_global_device_ids=true, to_apply=%region_12.0 | all-reduce | flops 145 | bytes 1160 | tf_op jit(solution)/shard_map/psum | solution.py:114
  298.3 7.6 %concatenate.1 = f32[77,6144]{1,0:T(8,128)} concatenate(f32[21,6144]{1,0:T(8,128)} %collective-permute-done.1, f32[56,6144]{1,0:T(8,128)S(1)} %fusion.1), dimensions={0} | concatenate | bytes 3784704
  306.0 1.7 fusion.49
  309.6 1.5 convert_reduce_fusion.3
  311.2 41.1 %all-reduce.5 = (f32[768]{0:T(1024)}, f32[768]{0:T(1024)}, f32[768]{0:T(1024)}, f32[768]{0:T(1024)}, f32[3072]{0:T(1024)S(1)}, /*index=5*/f32[768]{0:T(1024)}) all-reduce(f32[768]{0:T(1024)S(1)} %get-tuple-element.16, f32[768]{0:T(1024)S(1)} %reduce_sum.205, ...), channel_id=1, replica_groups=mesh['dp'=8,'tensor'=4] {'dp','tensor'}, use_global_device_ids=true, to_apply=%region_18.0 | all-reduce | flops 6912 | bytes 55296 | tf_op jit(solution)/shard_map/psum | solution.py:117
  352.9 52.7 %reduce-scatter.9.cloned.1.call-done = f32[96,768]{1,0:T(8,128)} async-done(((f32[3072,768]{1,0:T(8,128)}), f32[96,768]{1,0:T(8,128)}) %reduce-scatter.9.cloned.1.call-update) | async-done | bytes 294928 | tf_op jit(solution)/shard_map/reduce_scatter | solution.py:123
  405.5 140.9 %reduce-scatter.7.cloned.1.call-done = f32[768,96]{0,1:T(8,128)} async-done(((f32[768,3072]{0,1:T(8,128)}), f32[768,96]{0,1:T(8,128)}) %reduce-scatter.7.cloned.1.call-update) | async-done | bytes 294928 | tf_op jit(solution)/shard_map/reduce_scatter | solution.py:122
  546.5 1.5 copy.34
  548.0 1.5 copy.35
  (103 shorter events, 6.9 us)
Async XLA Ops:
  7.2 40.2 %copy-start = (bf16[96,196]{1,0:T(8,128)(2,1)S(1)}, bf16[96,196]{1,0:T(8,128)(2,1)}, u32[]{:S(2)}) copy-start(bf16[96,196]{1,0:T(8,128)(2,1)} %param.19) | copy-start | bytes 112900
  7.2 6.6 %copy-start.22 = (bf16[96]{0:T(256)(128)(2,1)S(1)}, bf16[96]{0:T(256)(128)(2,1)}, u32[]{:S(2)}) copy-start(bf16[96]{0:T(256)(128)(2,1)} %param.18) | copy-start | bytes 580
  7.2 35.7 %all-gather.5.cloned.1.call-start = ((), (), s32[]{:S(2)}) async-start(), calls=%async_computation.4 | async-start | bytes 3440640 | tf_op jit(solution)/shard_map/all_gather | solution.py:39
  13.8 164.6 %all-gather.7.cloned.1.call-start = ((), (), s32[]{:S(2)}) async-start(), calls=%async_computation.5 | async-start | bytes 3440640 | tf_op jit(solution)/shard_map/all_gather | solution.py:88
  13.8 31.6 %copy-start.16 = (bf16[196,96]{0,1:T(8,128)(2,1)S(1)}, bf16[196,96]{0,1:T(8,128)(2,1)}, u32[]{:S(2)}) copy-start(bf16[196,96]{0,1:T(8,128)(2,1)} %param.17) | copy-start | bytes 112900
  46.0 1.5 copy-start.3
  50.6 55.7 %copy-start.23 = (bf16[49]{0:T(256)(128)(2,1)S(1)}, bf16[49]{0:T(256)(128)(2,1)}, u32[]{:S(2)}) copy-start(bf16[49]{0:T(256)(128)(2,1)} %param.20) | copy-start | bytes 298
  50.6 55.7 %copy-start.18 = (bf16[768]{0:T(1024)(128)(2,1)S(1)}, bf16[768]{0:T(1024)(128)(2,1)}, u32[]{:S(2)}) copy-start(bf16[768]{0:T(1024)(128)(2,1)} %param.23) | copy-start | bytes 4612
  50.6 55.7 %copy-start.19 = (bf16[768]{0:T(1024)(128)(2,1)S(1)}, bf16[768]{0:T(1024)(128)(2,1)}, u32[]{:S(2)}) copy-start(bf16[768]{0:T(1024)(128)(2,1)} %param.24) | copy-start | bytes 4612
  50.6 55.7 %copy-start.17 = (bf16[3072]{0:T(1024)(128)(2,1)S(1)}, bf16[3072]{0:T(1024)(128)(2,1)}, u32[]{:S(2)}) copy-start(bf16[3072]{0:T(1024)(128)(2,1)} %param.26) | copy-start | bytes 18436
  50.6 55.9 %copy-start.21 = (u32[32]{0:T(128)S(1)}, u32[32]{0:T(128)}, u32[]{:S(2)}) copy-start(u32[32]{0:T(128)} %constant.43) | copy-start | bytes 388
  103.5 4.2 collective-permute-start
  118.8 4.3 copy-start.2
  123.9 7.1 %slice-start.2 = ((s8[4718592]{0:T(1024)(128)(4,1)}), s8[4194304]{0:T(1024)(128)(4,1)S(1)}, s32[]{:S(2)}) async-start(s8[4718592]{0:T(1024)(128)(4,1)} %bitcast.90), calls=%async_computation.9 | async-start | bytes 8388608
  125.6 0.8 copy-start.14
  126.4 4.5 copy-start.12
  126.4 4.6 slice-start.3
  126.4 10.0 %slice-start = ((s8[4718592]{0:T(1024)(128)(4,1)}), s8[4194304]{0:T(1024)(128)(4,1)S(1)}, s32[]{:S(2)}) async-start(s8[4718592]{0:T(1024)(128)(4,1)} %bitcast.88), calls=%async_computation.7 | async-start | bytes 8388608
  131.0 5.4 copy-start.25
  131.0 5.4 copy-start.5
  131.0 5.4 slice-start.1
  136.4 2.5 copy-start.24
  139.5 1.1 copy-start.7
  144.0 208.9 %all-reduce.10.cloned.1.call-start = ((), (), s32[]{:S(2)}) async-start(), calls=%async_computation.6 | async-start | bytes 393216 | tf_op jit(solution)/shard_map/psum | solution.py:114
  182.4 4.3 copy-start.4
  182.4 4.3 copy-start.11
  188.8 1.0 copy-start.9
  191.6 213.9 %reduce-scatter.9.cloned.1.call-start = ((), (), s32[]{:S(2)}) async-start(), calls=%async_computation.3 | async-start | bytes 9732096 | tf_op jit(solution)/shard_map/reduce_scatter | solution.py:123
  201.0 1.1 copy-start.15
  201.0 345.4 %reduce-scatter.7.cloned.1.call-start = ((), (), s32[]{:S(2)}) async-start(), calls=%async_computation.2 | async-start | bytes 9732096 | tf_op jit(solution)/shard_map/reduce_scatter | solution.py:122
  210.1 0.7 copy-start.20
  210.1 1.3 copy-start.10
  214.4 54.2 %copy-start.6 = (f32[392,768]{1,0:T(8,128)S(1)}, f32[392,768]{1,0:T(8,128)}, u32[]{:S(2)}) copy-start(f32[392,768]{1,0:T(8,128)} %reshape.158) | copy-start | bytes 3612676
  266.3 32.1 %collective-permute-start.1 = (f32[21,6144]{1,0:T(8,128)}, f32[21,6144]{1,0:T(8,128)}, u32[]{:S(2)}, u32[]{:S(2)}) collective-permute-start(f32[21,6144]{1,0:T(8,128)} %slice.1), channel_id=1, source_target_pairs={{0,1},{1,2},{2,3},{4,5},{5,6},{6,7},{8,9},{9,10},{10,11},{12,13},{... | collective-permute-start | bytes 1548296
  308.1 1.3 copy-start.8
  308.1 1.5 copy-start.13
  309.2 240.4 %copy-start.1 = (bf16[96,196]{1,0:T(8,128)(2,1)S(1)}, bf16[96,196]{1,0:T(8,128)(2,1)}, u32[]{:S(2)}) copy-start(bf16[96,196]{1,0:T(8,128)(2,1)} %param.19) | copy-start | bytes 112900
Sparse Core Ops, SparseCore 0:
  13.9 28.9 all-gather.4
  144.1 34.2 all-gather.6
  191.7 70.1 all-reduce.9
  269.3 136.2 reduce-scatter.8
  411.8 134.5 reduce-scatter.6
where the time goes:
time: 558 us; the launch traced here: 556 us
  waiting for transfers between devices  257 us (46%)
  blocking collectives  166 us (30%)
  matrix products  52.2 us (9%)
  local copies, waits for them, and re-layouts  44.1 us (8%)
  other arithmetic  16.5 us (3%)
  between operations  15.6 us (3%)
    reduce_scatter x1, waiting for transfers between devices, local(): lax.psum_scatter(broaden_grad, ('dp', 'tensor'), scatter_dimension=1, til...  141 us
    unnamed x2, blocking collectives  103 us
    reduce_scatter x1, waiting for transfers between devices, local(): lax.psum_scatter(narrow_grad, ('dp', 'tensor'), scatter_dimension=0, tile...  52.7 us
    unnamed x74, local copies, waits for them, and re-layouts  41.2 us
    psum x1, blocking collectives, local(): lax.psum((lowering_grad, scaling_grad, centering_grad, rescaling_grad, re...  41.1 us
    all_gather x1, waiting for transfers between devices, local(): mixed_all = lax.all_gather(mixed_low, 'tensor', axis=0, tiled=True)  34.2 us
    all_gather x1, waiting for transfers between devices, local(): normed_all = lax.all_gather(normed_local, 'tensor', axis=0, tiled=True)  29.1 us
    psum x1, blocking collectives, local(): lax.psum((expand_grad, uplift_grad, contract_grad, offset_grad), 'dp')  22 us
  transfers between devices with their start and end apart: 7, of which 4 were waited for; matrix products, arithmetic and copies ran while one was open for 17% of the time, Pallas kernels for 0%

commit v1 on v0

--- a/solution.py
+++ b/solution.py
@@ -2,6 +2,7 @@
 import jax.numpy as jnp
 from jax import lax
 from jax.sharding import PartitionSpec as P
+from jax.lax import axis_index, axis_size, ppermute
 
 
 def layer_norm(values, scale_vec, shift_vec):
@@ -36,7 +37,29 @@
         layer_norm, input_float, scaling.astype(jnp.float32), centering.astype(jnp.float32)
     )
     normed_local = normed_first.astype(jnp.bfloat16).reshape(part_rows, columns)
-    normed_all = lax.all_gather(normed_local, "tensor", axis=0, tiled=True)
+    back, w1, oldest = (axis_size("tensor"), axis_index("tensor"), normed_local.shape[0])
+    normed_all = lax.dynamic_update_slice_in_dim(
+        jnp.zeros(
+            [k0 * back if hop_no == 0 else k0 for hop_no, k0 in enumerate(normed_local.shape)],
+            normed_local.dtype,
+        ),
+        normed_local,
+        w1 * oldest,
+        axis=0,
+    )
+    y2 = block_out = normed_local
+    for i in range(1, back // 2 + 1):
+        y2 = ppermute(y2, "tensor", [(hop_no, (hop_no + 1) % back) for hop_no in range(back)])
+        normed_all = lax.dynamic_update_slice_in_dim(
+            normed_all, y2, (w1 - i) % back * oldest, axis=0
+        )
+        if 2 * i < back:
+            block_out = ppermute(
+                block_out, "tensor", perm=[(hop_no, (hop_no - 1) % back) for hop_no in range(back)]
+            )
+            normed_all = lax.dynamic_update_slice_in_dim(
+                normed_all, block_out, (w1 + i) % back * oldest, axis=0
+            )
     token_pre = (
         jnp.einsum("sj,sn->jn", expand, normed_all, preferred_element_type=jnp.float32)
         + uplift.astype(jnp.float32)[:, None]

time: 558 us -> 501 us (0.90)
  waiting for transfers between devices: 257 us -> 170 us
  local copies, waits for them, and re-layouts: 44.1 us -> 59 us
  blocking collectives: 166 us -> 174 us
    reduce_scatter x1, waiting for transfers between devices: 52.7 us -> 0.01 us  [local(): lax.psum_scatter(narrow_grad, ('dp', 'tensor'), scatter_dimension=0, tile...]
    all_gather x1 -> x0, waiting for transfers between devices: 29.1 us -> none  [local(): normed_all = lax.all_gather(normed_local, 'tensor', axis=0, tiled=True)]
    dynamic_update_slice x0 -> x4, local copies, waits for them, and re-layouts: none -> 17.2 us  [the longest x2 8.46 us: local(): lax.dynamic_update_slice_in_dim(normed_all, y2, (w1 - i) % back * oldest,...]
    reduce_scatter x1, waiting for transfers between devices: 141 us -> 124 us  [local(): lax.psum_scatter(broaden_grad, ('dp', 'tensor'), scatter_dimension=1, til...]
    ppermute x0 -> x3, waiting for transfers between devices: none -> 13.6 us  [the longest x2 13.6 us: local(): ppermute(y2, 'tensor', [(hop_no, (hop_no + 1) % back) for hop_no in range...]
    unnamed x2, blocking collectives: 103 us -> 114 us
  transfers between devices with their start and end apart: 7 -> 9, of which waited for: 4 -> 3; matrix products, arithmetic and copies ran while one was open for 17% -> 23% of each run, Pallas kernels for 0% -> 0%
where the time goes in v1:
time: 501 us; the launch traced here: 499 us
  blocking collectives  174 us (35%)
  waiting for transfers between devices  170 us (34%)
  local copies, waits for them, and re-layouts  59 us (12%)
  matrix products  52.6 us (10%)
  between operations  17.4 us (3%)
  other arithmetic  16.5 us (3%)
  starting transfers between devices  9.82 us (2%)
    reduce_scatter x1, waiting for transfers between devices, local(): lax.psum_scatter(broaden_grad, ('dp', 'tensor'), scatter_dimension=1, til...  124 us
    unnamed x2, blocking collectives  114 us
    unnamed x74, local copies, waits for them, and re-layouts  38.5 us
    psum x1, blocking collectives, local(): lax.psum((lowering_grad, scaling_grad, centering_grad, rescaling_grad, re...  38.3 us
    all_gather x1, waiting for transfers between devices, local(): mixed_all = lax.all_gather(mixed_low, 'tensor', axis=0, tiled=True)  32.5 us
    psum x1, blocking collectives, local(): lax.psum((expand_grad, uplift_grad, contract_grad, offset_grad), 'dp')  22 us
    ppermute x2, waiting for transfers between devices, local(): ppermute(y2, 'tensor', [(hop_no, (hop_no + 1) % back) for hop_no in range...  13.6 us
  transfers between devices with their start and end apart: 9, of which 3 were waited for; matrix products, arithmetic and copies ran while one was open for 23% of the time, Pallas kernels for 0%

profile of v1, /device:TPU:0, one launch (start us, length us, event | category | flops | bytes accessed | tf_op | source)
XLA Modules:
  0.0 499.0 jit_solution(1580848197127059805)
XLA Ops:
  9.4 1.2 convert_reduce_fusion.2
  10.7 1.4 fusion.34
  12.1 1.4 fusion.28
  13.5 1.0 copy.29
  14.9 1.9 collective-permute-start.1
  16.8 13.6 %collective-permute-done = bf16[49,6144]{1,0:T(8,128)(2,1)} collective-permute-done((bf16[49,6144]{1,0:T(8,128)(2,1)}, bf16[49,6144]{1,0:T(8,128)(2,1)}, u32[]{:S(2)}, u32[]{:S(2)}) %collective-permute-start) | collective-permute-done | bytes 602144 | tf_op jit(solution)/shard_map/ppermute | solution.py:52
  30.5 2.6 collective-permute-start.2
  33.3 4.4 dynamic_update_slice.12
  37.8 4.1 dynamic_update_slice.13
  41.8 4.4 dynamic_update_slice.14
  46.2 4.4 dynamic_update_slice.15
  51.1 1.4 copy-done.3
  52.6 3.1 convolution_bitcast_fusion.1
  55.8 54.0 %fusion = f32[56,6144]{1,0:T(8,128)} fusion(f32[196,6144]{1,0:T(8,128)} %convolution_bitcast_fusion.1), kind=kCustom, calls=%all-reduce-scatter | all-reduce-scatter fusion | flops 1376257 | bytes 6193664
  109.8 1.1 slice
  110.9 2.1 collective-permute-start.3
  115.1 8.4 %concatenate = f32[77,6144]{1,0:T(8,128)} concatenate(f32[21,6144]{1,0:T(8,128)} %collective-permute-done.3, f32[56,6144]{1,0:T(8,128)} %fusion), dimensions={0} | concatenate | bytes 3784704
  123.5 2.7 dynamic-slice_add_fusion
  126.2 2.6 reshape.158
  128.8 1.8 copy.30
  131.2 1.7 add_convert_fusion
  133.8 4.5 fusion.52
  138.4 5.5 %convert_reduce_fusion = (f32[3072]{0:T(1024)S(1)}, bf16[392,3072]{1,0:T(8,128)(2,1)S(1)}) fusion(f32[392,3072]{1,0:T(8,128)S(1)} %fusion.52, f32[3072]{0:T(1024)S(1)} %convert_element_type.94, bf16[3072,768]{1,0:T(8,128)(2,1)S(1)} %bitcast.95, bf16[49,8,768]{2,1,0:T(8,128)(2,1)S(1)} %copy-done.12, f32[392]{0:T(512)S(1)} %mul.256), kind=kOutput, calls=%fused_computation.14 | convolution fusion | flops 1878285312 | bytes 12572192 | tf_op jit(solution)/shard_map/rd,kd->rk/dot_general | solution.py:101
  144.0 2.4 multiply_reduce_fusion
  147.1 1.1 copy-done.7
  148.1 1.1 convert_reduce_fusion.4
  149.3 2.2 reshape.165
  151.8 32.5 %all-gather.3.cloned.1.call-done = bf16[4,49,6144]{2,1,0:T(8,128)(2,1)} async-done(((bf16[1,49,6144]{2,1,0:T(8,128)(2,1)}), bf16[4,49,6144]{2,1,0:T(8,128)(2,1)}) %all-gather.3.cloned.1.call-update) | async-done | bytes 2408464 | tf_op jit(solution)/shard_map/all_gather | solution.py:111
  184.2 4.0 reshape.166
  188.2 4.3 fusion.48
  192.5 2.1 convert_reduce_fusion.1
  194.6 1.0 copy-done.9
  195.7 1.7 fusion.53
  197.4 9.3 %fusion.41 = f32[3072,768]{1,0:T(8,128)} fusion(bf16[49,8,768]{2,1,0:T(8,128)(2,1)} %param.29, f32[392]{0:T(512)S(1)} %mul.256, f32[392,3072]{1,0:T(8,128)} %copy-done.25, f32[3072]{0:T(1024)S(1)} %convert_element_type.94), kind=kOutput, calls=%fused_computation.69 | convolution fusion | flops 1862633472 | bytes 14870048 | tf_op jit(solution)/shard_map/rk,rd->kd/dot_general | solution.py:99
  206.8 1.0 copy-done.15
  207.8 8.0 %fusion.54 = f32[768,3072]{0,1:T(8,128)} fusion(bf16[392,768]{1,0:T(8,128)(2,1)S(1)} %copy-done.15, bf16[392,3072]{1,0:T(8,128)(2,1)} %copy-done.24), kind=kOutput, calls=%fused_computation.87 | convolution fusion | flops 1849688064 | bytes 12447744 | tf_op jit(solution)/shard_map/rd,rk->dk/dot_general | solution.py:104
  217.2 3.1 convolution_bitcast_fusion
  220.3 59.5 %fusion.1 = f32[56,6144]{1,0:T(8,128)S(1)} fusion(f32[196,6144]{1,0:T(8,128)} %convolution_bitcast_fusion), kind=kCustom, calls=%all-reduce-scatter.1 | all-reduce-scatter fusion | flops 1376257 | bytes 6193664
  280.6 2.4 collective-permute-start.4
  283.0 8.1 %fusion.26 = bf16[49,8,768]{2,1,0:T(8,128)(2,1)} fusion(bf16[3072,768]{1,0:T(8,128)(2,1)} %param.27, f32[392]{0:T(512)S(1)} %mul.256, f32[768]{0:T(1024)S(1)} %convert_element_type.96, f32[392,768]{1,0:T(8,128)S(1)} %copy-done.6, bf16[49,8,768]{2,1,0:T(8,128)(2,1)S(1)} %copy-done.2, f32[392,3072]{1,0:T(8,128)} %copy-done.25, f32[3072]{0:T(1024)S(1)} %convert_element_type.94), kind=kOutput, calls=%fused_computation.46 | convolution fusion | flops 1863536640 | bytes 11960864 | tf_op jit(solution)/shard_map/dot_general | solution.py:89
  291.0 22.0 %all-reduce.6 = (f32[96]{0:T(128)}, f32[49]{0:T(128)}) all-reduce(f32[96]{0:T(128)S(1)} %get-tuple-element.38, f32[49]{0:T(128)S(1)} %reduce_sum.201), channel_id=1, replica_groups=mesh['dp'=8,'tensor'=4] {'dp'}, use_global_device_ids=true, to_apply=%region_12.13 | all-reduce | flops 145 | bytes 1160 | tf_op jit(solution)/shard_map/psum | solution.py:137
  313.0 7.6 %concatenate.1 = f32[77,6144]{1,0:T(8,128)} concatenate(f32[21,6144]{1,0:T(8,128)} %collective-permute-done.4, f32[56,6144]{1,0:T(8,128)S(1)} %fusion.1), dimensions={0} | concatenate | bytes 3784704
  320.7 1.7 fusion.49
  324.2 1.5 convert_reduce_fusion.3
  325.8 38.3 %all-reduce.5 = (f32[768]{0:T(1024)}, f32[768]{0:T(1024)}, f32[768]{0:T(1024)}, f32[768]{0:T(1024)}, f32[3072]{0:T(1024)S(1)}, /*index=5*/f32[768]{0:T(1024)}) all-reduce(f32[768]{0:T(1024)S(1)} %get-tuple-element.16, f32[768]{0:T(1024)S(1)} %reduce_sum.205, ...), channel_id=1, replica_groups=mesh['dp'=8,'tensor'=4] {'dp','tensor'}, use_global_device_ids=true, to_apply=%region_18.19 | all-reduce | flops 6912 | bytes 55296 | tf_op jit(solution)/shard_map/psum | solution.py:140
  364.6 123.8 %reduce-scatter.7.cloned.1.call-done = f32[768,96]{0,1:T(8,128)} async-done(((f32[768,3072]{0,1:T(8,128)}), f32[768,96]{0,1:T(8,128)}) %reduce-scatter.7.cloned.1.call-update) | async-done | bytes 294928 | tf_op jit(solution)/shard_map/reduce_scatter | solution.py:145
  488.5 1.5 copy.39
  490.0 1.5 copy.40
  (111 shorter events, 10.7 us)
Async XLA Ops:
  8.0 44.6 %copy-start = (bf16[96,196]{1,0:T(8,128)(2,1)S(1)}, bf16[96,196]{1,0:T(8,128)(2,1)}, u32[]{:S(2)}) copy-start(bf16[96,196]{1,0:T(8,128)(2,1)} %param.19) | copy-start | bytes 112900
  8.0 176.2 %all-gather.3.cloned.1.call-start = ((), (), s32[]{:S(2)}) async-start(), calls=%async_computation.4 | async-start | bytes 3440640 | tf_op jit(solution)/shard_map/all_gather | solution.py:111
  10.7 22.4 %copy-start.22 = (bf16[96]{0:T(256)(128)(2,1)S(1)}, bf16[96]{0:T(256)(128)(2,1)}, u32[]{:S(2)}) copy-start(bf16[96]{0:T(256)(128)(2,1)} %param.18) | copy-start | bytes 580
  14.5 16.0 %collective-permute-start = (bf16[49,6144]{1,0:T(8,128)(2,1)}, bf16[49,6144]{1,0:T(8,128)(2,1)}, u32[]{:S(2)}, u32[]{:S(2)}) collective-permute-start(bf16[49,6144]{1,0:T(8,128)(2,1)} %bitcast.16), channel_id=1, source_target_pairs={{0,1},{1,2},{2,3},{3,0},{4,5},{5,6},{6,7},{7,4},{8,9},{9,10},{10,1... | collective-permute-start | bytes 1806344 | tf_op jit(solution)/shard_map/ppermute | solution.py:52
  14.9 26.9 %collective-permute-start.1 = (bf16[49,6144]{1,0:T(8,128)(2,1)}, bf16[49,6144]{1,0:T(8,128)(2,1)}, u32[]{:S(2)}, u32[]{:S(2)}) collective-permute-start(bf16[49,6144]{1,0:T(8,128)(2,1)} %bitcast.16), channel_id=1, source_target_pairs={{0,3},{1,0},{2,1},{3,2},{4,7},{5,4},{6,5},{7,6},{8,11},{9,8},{10,9... | collective-permute-start | bytes 1806344 | tf_op jit(solution)/shard_map/ppermute | solution.py:57
  30.5 15.7 %collective-permute-start.2 = (bf16[49,6144]{1,0:T(8,128)(2,1)}, bf16[49,6144]{1,0:T(8,128)(2,1)}, u32[]{:S(2)}, u32[]{:S(2)}) collective-permute-start(bf16[49,6144]{1,0:T(8,128)(2,1)} %collective-permute-done), channel_id=1, source_target_pairs={{0,1},{1,2},{2,3},{3,0},{4,5},{5,6},{6,7},{7,4},{8,9},{9,10},{10,1... | collective-permute-start | bytes 1806344 | tf_op jit(solution)/shard_map/ppermute | solution.py:52
  37.7 12.9 %copy-start.16 = (bf16[196,96]{0,1:T(8,128)(2,1)S(1)}, bf16[196,96]{0,1:T(8,128)(2,1)}, u32[]{:S(2)}) copy-start(bf16[196,96]{0,1:T(8,128)(2,1)} %param.17) | copy-start | bytes 112900
  51.1 1.5 copy-start.3
  55.7 57.9 %copy-start.23 = (bf16[49]{0:T(256)(128)(2,1)S(1)}, bf16[49]{0:T(256)(128)(2,1)}, u32[]{:S(2)}) copy-start(bf16[49]{0:T(256)(128)(2,1)} %param.20) | copy-start | bytes 298
  55.7 57.9 %copy-start.18 = (bf16[768]{0:T(1024)(128)(2,1)S(1)}, bf16[768]{0:T(1024)(128)(2,1)}, u32[]{:S(2)}) copy-start(bf16[768]{0:T(1024)(128)(2,1)} %param.23) | copy-start | bytes 4612
  55.7 58.0 %copy-start.19 = (bf16[768]{0:T(1024)(128)(2,1)S(1)}, bf16[768]{0:T(1024)(128)(2,1)}, u32[]{:S(2)}) copy-start(bf16[768]{0:T(1024)(128)(2,1)} %param.24) | copy-start | bytes 4612
  55.7 58.0 %copy-start.17 = (bf16[3072]{0:T(1024)(128)(2,1)S(1)}, bf16[3072]{0:T(1024)(128)(2,1)}, u32[]{:S(2)}) copy-start(bf16[3072]{0:T(1024)(128)(2,1)} %param.26) | copy-start | bytes 18436
  55.7 58.1 %copy-start.21 = (u32[32]{0:T(128)S(1)}, u32[32]{0:T(128)}, u32[]{:S(2)}) copy-start(u32[32]{0:T(128)} %constant.82) | copy-start | bytes 388
  110.9 4.2 collective-permute-start.3
  126.2 4.3 copy-start.2
  131.2 7.1 %slice-start.2 = ((s8[4718592]{0:T(1024)(128)(4,1)}), s8[4194304]{0:T(1024)(128)(4,1)S(1)}, s32[]{:S(2)}) async-start(s8[4718592]{0:T(1024)(128)(4,1)} %bitcast.94), calls=%async_computation.8 | async-start | bytes 8388608
  133.0 0.8 copy-start.14
  133.8 4.6 copy-start.12
  133.8 4.6 slice-start.3
  133.8 10.1 %slice-start = ((s8[4718592]{0:T(1024)(128)(4,1)}), s8[4194304]{0:T(1024)(128)(4,1)S(1)}, s32[]{:S(2)}) async-start(s8[4718592]{0:T(1024)(128)(4,1)} %bitcast.92), calls=%async_computation.6 | async-start | bytes 8388608
  138.4 5.5 %copy-start.25 = (f32[392,3072]{1,0:T(8,128)}, f32[392,3072]{1,0:T(8,128)S(1)}, u32[]{:S(2)}) copy-start(f32[392,3072]{1,0:T(8,128)S(1)} %fusion.52) | copy-start | bytes 14450692
  138.4 5.5 %copy-start.5 = (f32[392,768]{1,0:T(8,128)S(1)}, f32[392,768]{1,0:T(8,128)}, u32[]{:S(2)}) copy-start(f32[392,768]{1,0:T(8,128)} %reshape.158) | copy-start | bytes 3612676
  138.4 5.5 %slice-start.1 = ((s8[4718592]{0:T(1024)(128)(4,1)}), s8[524288]{0:T(1024)(128)(4,1)S(1)}, s32[]{:S(2)}) async-start(s8[4718592]{0:T(1024)(128)(4,1)} %bitcast.92), calls=%async_computation.7 | async-start | bytes 1048576
  143.9 2.5 copy-start.24
  147.1 1.1 copy-start.7
  151.5 213.1 %all-reduce.10.cloned.1.call-start = ((), (), s32[]{:S(2)}) async-start(), calls=%async_computation.5 | async-start | bytes 393216 | tf_op jit(solution)/shard_map/psum | solution.py:137
  188.2 4.3 copy-start.4
  188.2 4.3 copy-start.11
  194.6 1.0 copy-start.9
  197.4 167.3 %reduce-scatter.9.cloned.1.call-start = ((), (), s32[]{:S(2)}) async-start(), calls=%async_computation.3 | async-start | bytes 9732096 | tf_op jit(solution)/shard_map/reduce_scatter | solution.py:146
  206.8 1.1 copy-start.15
  206.8 281.7 %reduce-scatter.7.cloned.1.call-start = ((), (), s32[]{:S(2)}) async-start(), calls=%async_computation.2 | async-start | bytes 9732096 | tf_op jit(solution)/shard_map/reduce_scatter | solution.py:145
  215.8 0.7 copy-start.20
  215.8 1.4 copy-start.10
  220.3 62.7 %copy-start.6 = (f32[392,768]{1,0:T(8,128)S(1)}, f32[392,768]{1,0:T(8,128)}, u32[]{:S(2)}) copy-start(f32[392,768]{1,0:T(8,128)} %reshape.158) | copy-start | bytes 3612676
  280.6 32.4 %collective-permute-start.4 = (f32[21,6144]{1,0:T(8,128)}, f32[21,6144]{1,0:T(8,128)}, u32[]{:S(2)}, u32[]{:S(2)}) collective-permute-start(f32[21,6144]{1,0:T(8,128)} %slice.1), channel_id=1, source_target_pairs={{0,1},{1,2},{2,3},{4,5},{5,6},{6,7},{8,9},{9,10},{10,11},{12,13},{... | collective-permute-start | bytes 1548296
  322.8 1.3 copy-start.8
  322.8 1.5 copy-start.13
  323.9 167.7 %copy-start.1 = (bf16[96,196]{1,0:T(8,128)(2,1)S(1)}, bf16[96,196]{1,0:T(8,128)(2,1)}, u32[]{:S(2)}) copy-start(bf16[96,196]{1,0:T(8,128)(2,1)} %param.19) | copy-start | bytes 112900
Sparse Core Ops, SparseCore 0:
  151.6 32.5 all-gather.2
  197.5 79.9 all-reduce.9
Sparse Core Ops, SparseCore 1:
  206.9 140.6 reduce-scatter.8
  353.8 134.6 reduce-scatter.6
